TPU v7x, 32 devices: a whole 2x2x4 slice. The times are simulated.
32 devices in a mesh: slab: 8 (over z, y), grp: 4 (over x, core).
Axes of the slice: x: 2, y: 2, z: 4, core: 2. Of those that a mesh axis runs over, the one named last changes fastest.
Arguments:
- positions: float32 [32, 3, 8192], P(('slab', 'grp')), may hold values from 0 to 1
- masses: float32 [32, 8192], P(('slab', 'grp')), may hold values from 0.001 to 0.01
- smoothing: float32 [32, 8192], P(('slab', 'grp')), may hold values from 0.3 to 0.6
- block_lists: int32 [32, 64, 8], P(('slab', 'grp')), may hold values from 0 to 63, as said below
- block_counts: int32 [32, 8], P(('slab', 'grp')), may hold values from 0 to 128, as said below
- group_owner: int32 [4, 8], P('grp'), may hold values from 0 to 7, each once within a row
Outputs:
- density: float32 [32, 8192], P(('slab', 'grp'))
- potential: float32 [32, 8192], P(('slab', 'grp'))
- group_energy: float32 [4, 8], P('grp', 'slab')
Inputs may be any that keep to these rules, and one draw needn't show every extreme that they name: `block_lists`: columns 0 to 1 name blocks of the slab below, the next 4 columns blocks of the own slab, the first of them the block itself, and the last 2 columns blocks of the slab above; the entries of each of these three sets differ. Block c of a slab lists block b of the slab below in its first 2 columns exactly when block b lists block c in its last 2 columns. `block_counts`: within one subgroup, a slab's rows begin with the members of its groups, group after group in order of group number. In every subgroup one group has 128 members on every slab.
All inputs are finite; a program needn't handle non-finite values.
Results may differ from a plain program's by a relative error of at most 0.0003.
Values sent between devices are 32-bit elements; how exact they have to be, the bound alone decides.
A program may use at most 64 MiB of HBM per device.

v0:
```python
import functools
import math

import jax
import jax.numpy as jnp
from jax import lax
from jax.experimental import pallas as pl
from jax.experimental.pallas import tpu as pltpu
from jax.sharding import PartitionSpec as P

TILE = 128
KX = 2
KO = 4
F32 = jnp.float32

DENSITY_SCALE = 21.0 / (2.0 * math.pi) / (64.0 * 256.0)

VMEM = pl.BlockSpec(memory_space=pltpu.VMEM)
MESH = pl.DeviceIdType.MESH
SMEM = pl.BlockSpec(memory_space=pltpu.SMEM)


def split3(a):
    high = a.astype(jnp.bfloat16).astype(F32)
    rest = a - high
    mid = rest.astype(jnp.bfloat16).astype(F32)
    return high, mid, rest - mid


def left_rows(a):
    high, mid, low = split3(a)
    return jnp.concatenate([high, high, mid, high, low, mid], axis=0).astype(jnp.bfloat16)


def right_rows(a):
    high, mid, low = split3(a)
    return jnp.concatenate([high, mid, high, low, high, mid], axis=0).astype(jnp.bfloat16)


def centred(particles, lift):
    row = lax.broadcasted_iota(jnp.int32, particles.shape, 0)
    shift = jnp.where(row == 0, lift - 0.5, jnp.where(row < 3, -0.5, 0.0))
    coords = jnp.where(row < 3, particles + shift, 0.0)
    norm = jnp.sum(coords * coords, axis=0, keepdims=True)
    return row, coords, norm


def source_features(particles, lift):
    row, coords, norm = centred(particles, lift)
    size = particles[4:5]
    return jnp.where(
        row < 3,
        coords,
        jnp.where(
            row == 3,
            norm,
            jnp.where(
                row == 4,
                1.0,
                jnp.where(row == 5, size, jnp.where(row == 6, size * size, 0.0)),
            ),
        ),
    )


def target_features(particles):
    row, coords, norm = centred(particles, 0.0)
    size = particles[4:5]
    distance = jnp.where(
        row < 3, -2.0 * coords, jnp.where(row == 3, 1.0, jnp.where(row == 4, norm, 0.0))
    )
    width = jnp.where(
        row == 4,
        size * size * 0.0625,
        jnp.where(row == 5, size * 0.125, jnp.where(row == 6, 0.0625, 0.0)),
    )
    return distance, width


def block_of(parts, i):
    place_ref, mass_ref, size_ref = parts
    row = lax.broadcasted_iota(jnp.int32, (8, TILE), 0)
    block = jnp.broadcast_to(size_ref[pl.ds(i, 1), :], (8, TILE))
    block = jnp.where(row == 3, mass_ref[pl.ds(i, 1), :], block)
    for axis in range(3):
        block = jnp.where(row == axis, place_ref[axis, pl.ds(i, 1), :], block)
    return block


def fill_targets(parts, target_ref):
    def step(i, _):
        distance, width = target_features(block_of(parts, i))
        target_ref[i] = left_rows(jnp.concatenate([distance, width], axis=1)).T
        return 0

    lax.fori_loop(0, target_ref.shape[0], step, 0, unroll=4)


def fill_sources(parts, source_ref, mass_ref, lift):
    def step(i, _):
        block = block_of(parts, i)
        source_ref[i] = right_rows(source_features(block, lift))
        mass_ref[i] = block[3:4]
        return 0

    lax.fori_loop(0, source_ref.shape[0], step, 0, unroll=4)


def pair_dot(left, right, left_dim=0):
    return lax.dot_general(
        left, right, (((left_dim,), (0,)), ((), ())), preferred_element_type=F32
    )


def weights(both_ref, k):
    squared = jnp.maximum(both_ref[pl.ds(2 * k * TILE, TILE), :], 1e-30)
    w = lax.rsqrt(both_ref[pl.ds((2 * k + 1) * TILE, TILE), :])
    t4 = squared * (lax.rsqrt(squared) * w)
    u = jnp.maximum(4.0 - t4, 0.0)
    a = w * (u * u)
    return (a * a) * (w * (1.0 + t4))


def sweep(first, last, fetch, use, even_ref, odd_ref):
    fetch(first, even_ref)

    def step(i, _):
        b = first + 2 * i
        fetch(b + 1, odd_ref)
        use(b, even_ref)
        fetch(jnp.minimum(b + 2, last - 1), even_ref)
        use(b + 1, odd_ref)
        return 0

    lax.fori_loop(0, (last - first) // 2, step, 0, unroll=4)


def fetcher(list_ref, first, width, target_ref, source_ref):
    def fetch(b, both_ref):
        target = target_ref[b]
        for k in range(width):
            both_ref[pl.ds(2 * k * TILE, 2 * TILE), :] = pair_dot(target, source_ref[list_ref[first + k, b]], 1)

    return fetch


def own_part(first, last, mass_ref, list_ref, dens_ref, target_ref, source_ref, even_ref, odd_ref):
    def use(b, both_ref):
        total = None
        for k in range(KO):
            term = weights(both_ref, k) * mass_ref[list_ref[KX + k, b]]
            total = term if total is None else total + term
        dens_ref[pl.ds(b, 1), :] += DENSITY_SCALE * jnp.sum(total, axis=1)[None, :]

    fetch = fetcher(list_ref, KX, KO, target_ref, source_ref)
    sweep(first, last, fetch, use, even_ref, odd_ref)


def cross_part(
    mass_ref, far_mass_ref, list_ref, dens_ref, column_ref, back_ref, target_ref, source_ref, even_ref, odd_ref
):
    blocks = mass_ref.shape[0]

    def use(b, both_ref):
        mass = jnp.broadcast_to(mass_ref[b], (TILE, TILE)).T
        total = None
        for k in range(KX):
            value = weights(both_ref, k)
            term = value * far_mass_ref[list_ref[KX + KO + k, b]]
            total = term if total is None else total + term
            column_ref[pl.ds(KX * b + k, 1), :] = DENSITY_SCALE * jnp.sum(value * mass, axis=0, keepdims=True)
        dens_ref[pl.ds(b, 1), :] += DENSITY_SCALE * jnp.sum(total.T, axis=0, keepdims=True)

    fetch = fetcher(list_ref, KX + KO, KX, target_ref, source_ref)
    sweep(0, blocks, fetch, use, even_ref, odd_ref)

    lane = lax.broadcasted_iota(jnp.int32, (1, KX * blocks), 1)

    def name(b, row):
        for k in range(KX):
            row = jnp.where(lane == KX * b + k, list_ref[KX + KO + k, b], row)
        return row

    named = lax.fori_loop(0, blocks, name, jnp.zeros((1, KX * blocks), jnp.int32), unroll=8)
    block = lax.broadcasted_iota(jnp.int32, (blocks, KX * blocks), 0)
    chosen = jnp.where(block == named, 1.0, 0.0)
    back_ref[...] = jnp.dot(
        chosen, column_ref[...], precision=lax.Precision.HIGHEST, preferred_element_type=F32
    )


def main_kernel(
    slabs,
    grps,
    place_ref,
    weight_ref,
    size_ref,
    group_ref,
    list_ref,
    dens_ref,
    table_ref,
    back_ref,
    energy_ref,
    far_place_ref,
    far_weight_ref,
    far_size_ref,
    member_ref,
    phi_ref,
    column_ref,
    sent_ref,
    target_ref,
    source_ref,
    far_ref,
    mass_ref,
    far_mass_ref,
    even_ref,
    odd_ref,
    near_even_ref,
    near_odd_ref,
    phi_target_ref,
    phi_source_ref,
    member_send,
    member_recv,
    phi_send,
    phi_recv,
    part_send,
    part_recv,
    back_send,
    back_recv,
):
    slab = lax.axis_index("slab")
    grp = lax.axis_index("grp")
    count = slabs * grps
    here = slab * grps + grp

    def place(index):
        return (index // grps, lax.rem(index, grps))

    above = place(lax.rem(here + 1, count))
    below = place(lax.rem(here + count - 1, count))

    def ahead(d):
        return lax.rem(slab + d, slabs)

    barrier = pltpu.get_barrier_semaphore()
    for other in (above, below):
        pl.semaphore_signal(barrier, inc=1, device_id=other, device_id_type=MESH)

    def greet(d, _):
        pl.semaphore_signal(barrier, inc=1, device_id=(ahead(d), grp), device_id_type=MESH)
        return 0

    lax.fori_loop(1, slabs, greet, 0)
    parts = (place_ref, weight_ref, size_ref)
    far_parts = (far_place_ref, far_weight_ref, far_size_ref)
    dens_ref[...] = jnp.zeros_like(dens_ref)
    fill_targets(parts, target_ref)
    fill_sources(parts, source_ref, mass_ref, 0.0)
    pl.semaphore_wait(barrier, slabs + 1)

    def member_copy(d):
        return pltpu.make_async_remote_copy(
            src_ref=group_ref.at[ahead(d)],
            dst_ref=member_ref.at[slab],
            send_sem=member_send.at[d],
            recv_sem=member_recv.at[d],
            device_id=(ahead(d), grp),
            device_id_type=MESH,
        )

    def phi_copy(d):
        return pltpu.make_async_remote_copy(
            src_ref=phi_ref.at[ahead(d)],
            dst_ref=table_ref.at[slab],
            send_sem=phi_send.at[d],
            recv_sem=phi_recv.at[d],
            device_id=(ahead(d), grp),
            device_id_type=MESH,
        )

    part_copies = [
        pltpu.make_async_remote_copy(
            src_ref=near,
            dst_ref=far,
            send_sem=part_send.at[n],
            recv_sem=part_recv.at[n],
            device_id=below,
            device_id_type=MESH,
        )
        for n, (near, far) in enumerate(zip(parts, far_parts))
    ]
    back_copy = pltpu.make_async_remote_copy(
        src_ref=sent_ref,
        dst_ref=back_ref,
        send_sem=back_send,
        recv_sem=back_recv,
        device_id=above,
        device_id_type=MESH,
    )

    def each(action):
        def step(d, _):
            action(d)
            return 0

        lax.fori_loop(1, slabs, step, 0)

    each(lambda d: member_copy(d).start())
    for copy in part_copies:
        copy.start()

    blocks = dens_ref.shape[0]
    half = blocks // 4 * 2
    own = (mass_ref, list_ref, dens_ref, target_ref, source_ref, even_ref, odd_ref)
    own_part(0, half, *own)

    member_ref[slab] = group_ref[slab]
    each(lambda d: member_copy(d).wait())
    phi_part(member_ref, phi_ref, energy_ref, phi_target_ref, phi_source_ref)
    each(lambda d: phi_copy(d).start())
    table_ref[slab] = phi_ref[slab]

    for copy in part_copies:
        copy.wait()
    fill_sources(far_parts, far_ref, far_mass_ref, 1.0)
    cross_part(
        mass_ref,
        far_mass_ref,
        list_ref,
        dens_ref,
        column_ref,
        sent_ref,
        target_ref,
        far_ref,
        near_even_ref,
        near_odd_ref,
    )
    back_copy.start()
    own_part(half, blocks, *own)
    each(lambda d: phi_copy(d).wait())
    back_copy.wait()


def pick_kernel(place_ref, weight_ref, size_ref, count_ref, owner_ref, out_ref):
    parts = (place_ref, weight_ref, size_ref)
    blocks = weight_ref.shape[0]
    row = lax.broadcasted_iota(jnp.int32, (8, TILE), 0)
    lane = lax.broadcasted_iota(jnp.int32, (8, TILE), 1)

    def step(k, start):
        count = count_ref[0, k]
        block = jnp.minimum(start // TILE, blocks - 1)
        shift = start % TILE
        after = jnp.minimum(block + 1, blocks - 1)
        first = block_of(parts, block)
        second = block_of(parts, after)
        mixed = pltpu.roll(jnp.where(lane >= shift, first, second), (TILE - shift) % TILE, 1)
        out_ref[owner_ref[0, k]] = jnp.where((row == 3) & (lane >= count), 0.0, mixed)
        return start + count

    lax.fori_loop(0, count_ref.shape[1], step, jnp.int32(0), unroll=8)


def phi_part(member_ref, phi_ref, energy_ref, target_ref, source_ref):
    slabs = member_ref.shape[0]
    group = math.gcd(slabs, 8)

    def fill(i, _):
        particles = member_ref[i]
        row, coords, norm = centred(particles, 0.0)
        size = particles[4:5]
        norm = norm + 0.125 * size * size
        base = pl.multiple_of(i * TILE, TILE)
        source_ref[:, pl.ds(base, TILE)] = right_rows(
            jnp.where(row < 3, coords, jnp.where(row == 3, norm, jnp.where(row == 4, 1.0, 0.0)))
        )
        target_ref[:, pl.ds(base, TILE)] = left_rows(
            jnp.where(row < 3, -2.0 * coords, jnp.where(row == 3, 1.0, jnp.where(row == 4, norm, 0.0)))
        )
        return 0

    lax.fori_loop(0, slabs, fill, 0)

    def step(i, energy):
        target = target_ref[:, pl.ds(pl.multiple_of(i * TILE, TILE), TILE)]

        def inner(j, total):
            for n in range(group):
                base = pl.multiple_of((j * group + n) * TILE, TILE)
                pairs = pair_dot(target, source_ref[:, pl.ds(base, TILE)])
                total = total + lax.rsqrt(pairs) * member_ref[j * group + n, 3:4, :]
            return total

        total = lax.fori_loop(0, slabs // group, inner, jnp.zeros((TILE, TILE), F32), unroll=slabs == group)
        mass = member_ref[i, 3:4, :]
        size = member_ref[i, 4:5, :]
        phi = mass * (2.0 / size) - jnp.sum(total.T, axis=0, keepdims=True)
        phi_ref[i] = phi
        return energy + mass * phi

    energy = lax.fori_loop(0, slabs, step, jnp.zeros((1, TILE), F32), unroll=4 if slabs == group else 1)
    energy_ref[...] = 0.5 * jnp.sum(energy, axis=1, keepdims=True)


def final_kernel(dens_ref, back_ref, table_ref, count_ref, owner_ref, out_ref, pot_ref, work_ref):
    out_ref[...] = dens_ref[...] + back_ref[...]
    work_ref[...] = jnp.zeros_like(work_ref)
    lane = lax.broadcasted_iota(jnp.int32, (1, TILE), 1)

    def step(k, start):
        count = count_ref[0, k]
        block = start // TILE
        shift = start % TILE
        value = table_ref[owner_ref[0, k]]
        value = pltpu.roll(jnp.where(lane < count, value, 0.0), shift, 1)
        work_ref[pl.ds(block, 1), :] += jnp.where(lane >= shift, value, 0.0)
        work_ref[pl.ds(block + 1, 1), :] += jnp.where(lane < shift, value, 0.0)
        return start + count

    lax.fori_loop(0, count_ref.shape[1], step, jnp.int32(0), unroll=8)
    pot_ref[...] = work_ref[: pot_ref.shape[0], :]


def per_device(positions, masses, smoothing, block_lists, block_counts, group_owner):
    row_count = masses.shape[1]
    blocks = row_count // TILE
    groups = block_counts.shape[1]
    slabs = lax.axis_size("slab")
    grps = lax.axis_size("grp")
    particles = (
        positions[0].reshape(3, blocks, TILE),
        masses.reshape(blocks, TILE),
        smoothing.reshape(blocks, TILE),
    )
    outgoing = pl.pallas_call(
        pick_kernel,
        out_shape=jax.ShapeDtypeStruct((groups, 8, TILE), F32),
        in_specs=[VMEM, VMEM, VMEM, SMEM, SMEM],
        out_specs=VMEM,
    )(*particles, block_counts, group_owner)

    grid_shape = jax.ShapeDtypeStruct((blocks, TILE), F32)
    row_shape = jax.ShapeDtypeStruct((slabs, 1, TILE), F32)
    half_type = jnp.bfloat16
    dma = pltpu.SemaphoreType.DMA
    density, table, back, energy = pl.pallas_call(
        functools.partial(main_kernel, slabs, grps),
        out_shape=(grid_shape, row_shape, grid_shape, jax.ShapeDtypeStruct((1, 1), F32)),
        in_specs=[VMEM, VMEM, VMEM, VMEM, SMEM],
        out_specs=(VMEM, VMEM, VMEM, VMEM),
        scratch_shapes=[
            pltpu.VMEM((3, blocks, TILE), F32),
            pltpu.VMEM((blocks, TILE), F32),
            pltpu.VMEM((blocks, TILE), F32),
            pltpu.VMEM((slabs, 8, TILE), F32),
            pltpu.VMEM((slabs, 1, TILE), F32),
            pltpu.VMEM((KX * blocks, TILE), F32),
            pltpu.VMEM((blocks, TILE), F32),
            pltpu.VMEM((blocks, 2 * TILE, 48), half_type),
            pltpu.VMEM((blocks, 48, TILE), half_type),
            pltpu.VMEM((blocks, 48, TILE), half_type),
            pltpu.VMEM((blocks, 1, TILE), F32),
            pltpu.VMEM((blocks, 1, TILE), F32),
            pltpu.VMEM((KO * 2 * TILE, TILE), F32),
            pltpu.VMEM((KO * 2 * TILE, TILE), F32),
            pltpu.VMEM((KX * 2 * TILE, TILE), F32),
            pltpu.VMEM((KX * 2 * TILE, TILE), F32),
            pltpu.VMEM((48, slabs * TILE), half_type),
            pltpu.VMEM((48, slabs * TILE), half_type),
            dma((slabs,)),
            dma((slabs,)),
            dma((slabs,)),
            dma((slabs,)),
            dma((3,)),
            dma((3,)),
            dma,
            dma,
        ],
        compiler_params=pltpu.CompilerParams(collective_id=0, has_side_effects=True),
    )(*particles, outgoing, block_lists[0].T)
    density, potential = pl.pallas_call(
        final_kernel,
        out_shape=(grid_shape, grid_shape),
        in_specs=[VMEM, VMEM, VMEM, SMEM, SMEM],
        out_specs=(VMEM, VMEM),
        scratch_shapes=[pltpu.VMEM((blocks + 8, TILE), F32)],
    )(density, back, table, block_counts, group_owner)
    return (density.reshape(1, row_count), potential.reshape(1, row_count), energy)


def solution(mesh):
    placed = (
        P(("slab", "grp"), None, None),
        P(("slab", "grp"), None),
        P(("slab", "grp"), None),
        P(("slab", "grp"), None, None),
        P(("slab", "grp"), None),
        P("grp", None),
    )
    return jax.shard_map(
        per_device,
        mesh=mesh,
        in_specs=placed,
        out_specs=(P(("slab", "grp"), None), P(("slab", "grp"), None), P("grp", "slab")),
        check_vma=False,
    )
```

profile of v0, /device:TPU:0, one launch (start us, length us, event | category | flops | bytes accessed | tf_op | source)
XLA Modules:
  0.0 35.8 jit_solution(17643852890399253590)
XLA Ops:
  0.6 1.7 %shard_map.85.group_ref = f32[8,8,128]{2,1,0:T(8,128)} custom-call(f32[3,64,128]{2,1,0:T(8,128)} %bitcast.8, f32[64,128]{1,0:T(8,128)} %bitcast.10, f32[64,128]{1,0:T(8,128)} %bitcast.12, s32[1,8]{1,0:T(1,128)} %count_ref.3, s32[1,8]{1,0:T(1,128)} %owner_ref.3), custom_call_target="tpu_custom_call" | custom-call | tf_op jit(solution)/shard_map/pallas_call | solution.py:435
  2.3 30.1 %shard_map.86 = (f32[64,128]{1,0:T(8,128)}, f32[8,1,128]{2,1,0:T(1,128)}, f32[64,128]{1,0:T(8,128)}, f32[1,1]{1,0:T(1,128)}) custom-call(f32[3,64,128]{2,1,0:T(8,128)} %bitcast.9, f32[64,128]{1,0:T(8,128)} %bitcast.11, f32[64,128]{1,0:T(8,128)} %bitcast.13, f32[8,8,128]{2,1,0:T(8,128)} %shard_map.85.group_ref, s32[8,64]{1,0:T(8,128)} %bitcast.14), custom_call_target="tpu_custom_call" | custom-call | tf_op jit(solution)/shard_map/pallas_call | solution.py:446
  32.4 1.6 %shard_map.87 = (f32[64,128]{1,0:T(8,128)}, f32[64,128]{1,0:T(8,128)}) custom-call(f32[64,128]{1,0:T(8,128)} %get-tuple-element.9.dens_ref, f32[64,128]{1,0:T(8,128)} %get-tuple-element.10.back_ref, f32[8,1,128]{2,1,0:T(1,128)} %get-tuple-element.11.table_ref, s32[1,8]{1,0:T(1,128)} %count_ref.3, s32[1,8]{1,0:T(1,128)} %owner_ref.3), custom_call_target="tpu_custom_call" | custom-call | tf_op jit(solution)/shard_map/pallas_call | solution.py:481
where the time goes:
time: 36.1 us; the launch traced here: 35.8 us
  Pallas kernels  33.4 us (93%)
  between operations  2.46 us (7%)
    pallas_call x1, Pallas kernels, per_device(): pl.pallas_call(functools.partial(main_kernel, slabs, grps), out_shape=(gr...  30.1 us
    pallas_call x1, Pallas kernels, per_device(): pl.pallas_call(pick_kernel, out_shape=jax.ShapeDtypeStruct((groups, 8, TI...  1.7 us
    pallas_call x1, Pallas kernels, per_device(): pl.pallas_call(final_kernel, out_shape=(grid_shape, grid_shape), in_specs...  1.56 us

commit v1 on v0

--- a/solution.py
+++ b/solution.py
@@ -12,8 +12,11 @@
 KX = 2
 KO = 4
 F32 = jnp.float32
-
-DENSITY_SCALE = 21.0 / (2.0 * math.pi) / (64.0 * 256.0)
+HALF = jnp.bfloat16
+DEPTH = 64
+LOT = 8
+
+DENSITY_SCALE = 21.0 / (256.0 * math.pi) / 16.0
 
 VMEM = pl.BlockSpec(memory_space=pltpu.VMEM)
 MESH = pl.DeviceIdType.MESH
@@ -21,20 +24,28 @@
 
 
 def split3(a):
-    high = a.astype(jnp.bfloat16).astype(F32)
+    high = a.astype(HALF).astype(F32)
     rest = a - high
-    mid = rest.astype(jnp.bfloat16).astype(F32)
+    mid = rest.astype(HALF).astype(F32)
     return high, mid, rest - mid
 
 
+def left_six(a):
+    high, mid, low = split3(a)
+    return [high, high, mid, high, low, mid]
+
+
+def right_six(a):
+    high, mid, low = split3(a)
+    return [high, mid, high, low, high, mid]
+
+
 def left_rows(a):
-    high, mid, low = split3(a)
-    return jnp.concatenate([high, high, mid, high, low, mid], axis=0).astype(jnp.bfloat16)
+    return jnp.concatenate(left_six(a), axis=0).astype(HALF)
 
 
 def right_rows(a):
-    high, mid, low = split3(a)
-    return jnp.concatenate([high, mid, high, low, high, mid], axis=0).astype(jnp.bfloat16)
+    return jnp.concatenate(right_six(a), axis=0).astype(HALF)
 
 
 def centred(particles, lift):
@@ -45,65 +56,68 @@
     return row, coords, norm
 
 
-def source_features(particles, lift):
-    row, coords, norm = centred(particles, lift)
-    size = particles[4:5]
-    return jnp.where(
-        row < 3,
-        coords,
-        jnp.where(
-            row == 3,
-            norm,
-            jnp.where(
-                row == 4,
-                1.0,
-                jnp.where(row == 5, size, jnp.where(row == 6, size * size, 0.0)),
-            ),
-        ),
-    )
-
-
-def target_features(particles):
-    row, coords, norm = centred(particles, 0.0)
-    size = particles[4:5]
-    distance = jnp.where(
-        row < 3, -2.0 * coords, jnp.where(row == 3, 1.0, jnp.where(row == 4, norm, 0.0))
-    )
-    width = jnp.where(
-        row == 4,
-        size * size * 0.0625,
-        jnp.where(row == 5, size * 0.125, jnp.where(row == 6, 0.0625, 0.0)),
-    )
-    return distance, width
-
-
-def block_of(parts, i):
+FACTORS = 8
+NORM, SIZE, PLANES = 8, 11, 14
+
+
+def fill_planes(parts, plane_ref, lift):
     place_ref, mass_ref, size_ref = parts
+
+    def step(i, _):
+        rows = pl.ds(pl.multiple_of(i * LOT, LOT), LOT)
+        coords = [place_ref[axis, rows, :] + ((lift if axis == 0 else 0.0) - 0.5) for axis in range(3)]
+        norm = coords[0] * coords[0] + coords[1] * coords[1] + coords[2] * coords[2]
+        size = size_ref[rows, :]
+        planes = coords + [lax.rsqrt(mass_ref[rows, :])]
+        for _ in range(4):
+            planes.append(planes[-1] * size)
+        planes += list(split3(norm)) + list(split3(size))
+        for n, plane in enumerate(planes):
+            plane_ref[n, rows, :] = plane
+        return 0
+
+    lax.fori_loop(0, mass_ref.shape[0] // LOT, step, 0, unroll=2)
+
+
+def by_row(values):
     row = lax.broadcasted_iota(jnp.int32, (8, TILE), 0)
-    block = jnp.broadcast_to(size_ref[pl.ds(i, 1), :], (8, TILE))
-    block = jnp.where(row == 3, mass_ref[pl.ds(i, 1), :], block)
-    for axis in range(3):
-        block = jnp.where(row == axis, place_ref[axis, pl.ds(i, 1), :], block)
+    block = jnp.broadcast_to(values[0], (8, TILE))
+    for n, value in enumerate(values[1:]):
+        block = jnp.where(row == n + 1, value, block)
     return block
 
 
-def fill_targets(parts, target_ref):
+def fill(parts, plane_ref, left_ref, right_ref, lift):
+    fill_planes(parts, plane_ref, lift)
+    row = lax.broadcasted_iota(jnp.int32, (8, TILE), 0)
+    zero = jnp.zeros((8, TILE), F32)
+
     def step(i, _):
-        distance, width = target_features(block_of(parts, i))
-        target_ref[i] = left_rows(jnp.concatenate([distance, width], axis=1)).T
+        plane = [plane_ref[n, pl.ds(i, 1), :] for n in range(PLANES)]
+        coords, powers, norm, size = plane[:3], plane[3:8], plane[NORM:SIZE], plane[SIZE:]
+        if left_ref is not None:
+            high, mid, low = split3(by_row(coords + powers[::-1]))
+            rest = by_row(norm + [1.0, 1.0, 1.0] + size[:2])
+            last = jnp.where(row == 0, size[2], 0.0)
+            left_ref[i] = jnp.concatenate([high, high, high, mid, mid, low, rest, last], axis=0).T.astype(HALF)
+        scale = by_row([-8.0, -8.0, -8.0, 0.0625, 0.25, 0.375, 0.25, 0.0625])
+        parts3 = split3(scale * by_row(coords + powers))
+        near = [jnp.where(row < 3, part, 0.0) for part in parts3]
+        far = [jnp.where(row < 3, 0.0, part) for part in parts3]
+        order = (0, 1, 2, 0, 1, 0)
+        rest = by_row([4.0, 4.0, 4.0] + [4.0 * part for part in norm] + [0.0, 0.0])
+        wide = by_row([0.0, 0.0, 0.0] + [2.0 * part for part in size] + [2.0, 2.0])
+        last = jnp.where(row == 0, 2.0, 0.0)
+        columns = (
+            [near[n] for n in order] + [rest, zero],
+            [zero] * 6 + [wide, last],
+            [far[n] for n in order] + [zero, zero],
+        )
+        for m, column in enumerate(columns):
+            right_ref[i, :, pl.ds(m * TILE, TILE)] = jnp.concatenate(column, axis=0).astype(HALF)
         return 0
 
-    lax.fori_loop(0, target_ref.shape[0], step, 0, unroll=4)
-
-
-def fill_sources(parts, source_ref, mass_ref, lift):
-    def step(i, _):
-        block = block_of(parts, i)
-        source_ref[i] = right_rows(source_features(block, lift))
-        mass_ref[i] = block[3:4]
-        return 0
-
-    lax.fori_loop(0, source_ref.shape[0], step, 0, unroll=4)
+    lax.fori_loop(0, right_ref.shape[0], step, 0, unroll=4)
 
 
 def pair_dot(left, right, left_dim=0):
@@ -113,15 +127,16 @@
 
 
 def weights(both_ref, k):
-    squared = jnp.maximum(both_ref[pl.ds(2 * k * TILE, TILE), :], 1e-30)
-    w = lax.rsqrt(both_ref[pl.ds((2 * k + 1) * TILE, TILE), :])
-    t4 = squared * (lax.rsqrt(squared) * w)
-    u = jnp.maximum(4.0 - t4, 0.0)
-    a = w * (u * u)
-    return (a * a) * (w * (1.0 + t4))
-
-
-def sweep(first, last, fetch, use, even_ref, odd_ref):
+    rows = pl.ds(k * TILE, TILE)
+    squared = jnp.maximum(both_ref[rows, :TILE], 1e-30)
+    reach = both_ref[rows, TILE : 2 * TILE]
+    near = jnp.maximum(reach - squared * lax.rsqrt(squared), 0.0)
+    a = near * lax.rsqrt(both_ref[rows, 2 * TILE : 3 * TILE])
+    a = a * a
+    return (a * a) * (1.25 * reach - near)
+
+
+def sweep(first, last, fetch, use, even_ref, odd_ref, unroll=4):
     fetch(first, even_ref)
 
     def step(i, _):
@@ -132,46 +147,40 @@
         use(b + 1, odd_ref)
         return 0
 
-    lax.fori_loop(0, (last - first) // 2, step, 0, unroll=4)
-
-
-def fetcher(list_ref, first, width, target_ref, source_ref):
+    lax.fori_loop(0, (last - first) // 2, step, 0, unroll=unroll)
+
+
+def own_part(first, last, list_ref, dens_ref, left_ref, right_ref, even_ref, odd_ref):
     def fetch(b, both_ref):
-        target = target_ref[b]
-        for k in range(width):
-            both_ref[pl.ds(2 * k * TILE, 2 * TILE), :] = pair_dot(target, source_ref[list_ref[first + k, b]], 1)
-
-    return fetch
-
-
-def own_part(first, last, mass_ref, list_ref, dens_ref, target_ref, source_ref, even_ref, odd_ref):
+        right = right_ref[b]
+        for k in range(KO):
+            both_ref[pl.ds(k * TILE, TILE), :] = pair_dot(left_ref[list_ref[KX + k, b]], right, 1)
+
     def use(b, both_ref):
-        total = None
+        total = jnp.zeros((8, TILE), F32)
         for k in range(KO):
-            term = weights(both_ref, k) * mass_ref[list_ref[KX + k, b]]
-            total = term if total is None else total + term
-        dens_ref[pl.ds(b, 1), :] += DENSITY_SCALE * jnp.sum(total, axis=1)[None, :]
-
-    fetch = fetcher(list_ref, KX, KO, target_ref, source_ref)
+            total = total + jnp.sum(weights(both_ref, k).reshape(TILE // 8, 8, TILE), axis=0)
+        dens_ref[pl.ds(b, 1), :] += jnp.sum(total, axis=0, keepdims=True)
+
     sweep(first, last, fetch, use, even_ref, odd_ref)
 
 
-def cross_part(
-    mass_ref, far_mass_ref, list_ref, dens_ref, column_ref, back_ref, target_ref, source_ref, even_ref, odd_ref
-):
-    blocks = mass_ref.shape[0]
+def cross_part(list_ref, dens_ref, column_ref, back_ref, left_ref, right_ref, even_ref, odd_ref):
+    blocks = left_ref.shape[0]
+
+    def fetch(b, both_ref):
+        left = left_ref[b]
+        for k in range(KX):
+            both_ref[pl.ds(k * TILE, TILE), :] = pair_dot(left, right_ref[list_ref[KX + KO + k, b]], 1)
 
     def use(b, both_ref):
-        mass = jnp.broadcast_to(mass_ref[b], (TILE, TILE)).T
         total = None
         for k in range(KX):
             value = weights(both_ref, k)
-            term = value * far_mass_ref[list_ref[KX + KO + k, b]]
-            total = term if total is None else total + term
-            column_ref[pl.ds(KX * b + k, 1), :] = DENSITY_SCALE * jnp.sum(value * mass, axis=0, keepdims=True)
-        dens_ref[pl.ds(b, 1), :] += DENSITY_SCALE * jnp.sum(total.T, axis=0, keepdims=True)
-
-    fetch = fetcher(list_ref, KX + KO, KX, target_ref, source_ref)
+            total = value if total is None else total + value
+            column_ref[pl.ds(KX * b + k, 1), :] = jnp.sum(value, axis=0, keepdims=True)
+        dens_ref[pl.ds(b, 1), :] += jnp.sum(total.T, axis=0, keepdims=True)
+
     sweep(0, blocks, fetch, use, even_ref, odd_ref)
 
     lane = lax.broadcasted_iota(jnp.int32, (1, KX * blocks), 1)
@@ -183,9 +192,10 @@
 
     named = lax.fori_loop(0, blocks, name, jnp.zeros((1, KX * blocks), jnp.int32), unroll=8)
     block = lax.broadcasted_iota(jnp.int32, (blocks, KX * blocks), 0)
-    chosen = jnp.where(block == named, 1.0, 0.0)
-    back_ref[...] = jnp.dot(
-        chosen, column_ref[...], precision=lax.Precision.HIGHEST, preferred_element_type=F32
+    chosen = jnp.where(block == named, 1.0, 0.0).astype(HALF)
+    high, mid, low = split3(column_ref[...])
+    back_ref[...] = sum(
+        jnp.dot(chosen, part.astype(HALF), preferred_element_type=F32) for part in (low, mid, high)
     )
 
 
@@ -208,17 +218,16 @@
     phi_ref,
     column_ref,
     sent_ref,
-    target_ref,
-    source_ref,
+    left_ref,
+    right_ref,
     far_ref,
-    mass_ref,
-    far_mass_ref,
     even_ref,
     odd_ref,
     near_even_ref,
     near_odd_ref,
     phi_target_ref,
     phi_source_ref,
+    plane_ref,
     member_send,
     member_recv,
     phi_send,
@@ -253,9 +262,13 @@
     lax.fori_loop(1, slabs, greet, 0)
     parts = (place_ref, weight_ref, size_ref)
     far_parts = (far_place_ref, far_weight_ref, far_size_ref)
+    blocks = dens_ref.shape[0]
+    early = blocks // 8 * 2
+    later = blocks // 4 * 2
+    own = (list_ref, dens_ref, left_ref, right_ref, even_ref, odd_ref)
     dens_ref[...] = jnp.zeros_like(dens_ref)
-    fill_targets(parts, target_ref)
-    fill_sources(parts, source_ref, mass_ref, 0.0)
+    fill(parts, plane_ref, left_ref, right_ref, 0.0)
+    own_part(0, early, *own)
     pl.semaphore_wait(barrier, slabs + 1)
 
     def member_copy(d):
@@ -309,10 +322,13 @@
     for copy in part_copies:
         copy.start()
 
-    blocks = dens_ref.shape[0]
-    half = blocks // 4 * 2
-    own = (mass_ref, list_ref, dens_ref, target_ref, source_ref, even_ref, odd_ref)
-    own_part(0, half, *own)
+    own_part(early, later, *own)
+
+    for copy in part_copies:
+        copy.wait()
+    fill(far_parts, plane_ref, None, far_ref, 1.0)
+    cross_part(list_ref, dens_ref, column_ref, sent_ref, left_ref, far_ref, near_even_ref, near_odd_ref)
+    back_copy.start()
 
     member_ref[slab] = group_ref[slab]
     each(lambda d: member_copy(d).wait())
@@ -320,25 +336,19 @@
     each(lambda d: phi_copy(d).start())
     table_ref[slab] = phi_ref[slab]
 
-    for copy in part_copies:
-        copy.wait()
-    fill_sources(far_parts, far_ref, far_mass_ref, 1.0)
-    cross_part(
-        mass_ref,
-        far_mass_ref,
-        list_ref,
-        dens_ref,
-        column_ref,
-        sent_ref,
-        target_ref,
-        far_ref,
-        near_even_ref,
-        near_odd_ref,
-    )
-    back_copy.start()
-    own_part(half, blocks, *own)
+    own_part(later, blocks, *own)
     each(lambda d: phi_copy(d).wait())
     back_copy.wait()
+
+
+def block_of(parts, i):
+    place_ref, mass_ref, size_ref = parts
+    row = lax.broadcasted_iota(jnp.int32, (8, TILE), 0)
+    block = jnp.broadcast_to(size_ref[pl.ds(i, 1), :], (8, TILE))
+    block = jnp.where(row == 3, mass_ref[pl.ds(i, 1), :], block)
+    for axis in range(3):
+        block = jnp.where(row == axis, place_ref[axis, pl.ds(i, 1), :], block)
+    return block
 
 
 def pick_kernel(place_ref, weight_ref, size_ref, count_ref, owner_ref, out_ref):
@@ -402,8 +412,8 @@
     energy_ref[...] = 0.5 * jnp.sum(energy, axis=1, keepdims=True)
 
 
-def final_kernel(dens_ref, back_ref, table_ref, count_ref, owner_ref, out_ref, pot_ref, work_ref):
-    out_ref[...] = dens_ref[...] + back_ref[...]
+def final_kernel(mass_ref, dens_ref, back_ref, table_ref, count_ref, owner_ref, out_ref, pot_ref, work_ref):
+    out_ref[...] = (dens_ref[...] + back_ref[...]) * (DENSITY_SCALE / mass_ref[...])
     work_ref[...] = jnp.zeros_like(work_ref)
     lane = lax.broadcasted_iota(jnp.int32, (1, TILE), 1)
 
@@ -441,7 +451,6 @@
 
     grid_shape = jax.ShapeDtypeStruct((blocks, TILE), F32)
     row_shape = jax.ShapeDtypeStruct((slabs, 1, TILE), F32)
-    half_type = jnp.bfloat16
     dma = pltpu.SemaphoreType.DMA
     density, table, back, energy = pl.pallas_call(
         functools.partial(main_kernel, slabs, grps),
@@ -456,17 +465,16 @@
             pltpu.VMEM((slabs, 1, TILE), F32),
             pltpu.VMEM((KX * blocks, TILE), F32),
             pltpu.VMEM((blocks, TILE), F32),
-            pltpu.VMEM((blocks, 2 * TILE, 48), half_type),
-            pltpu.VMEM((blocks, 48, TILE), half_type),
-            pltpu.VMEM((blocks, 48, TILE), half_type),
-            pltpu.VMEM((blocks, 1, TILE), F32),
-            pltpu.VMEM((blocks, 1, TILE), F32),
-            pltpu.VMEM((KO * 2 * TILE, TILE), F32),
-            pltpu.VMEM((KO * 2 * TILE, TILE), F32),
-            pltpu.VMEM((KX * 2 * TILE, TILE), F32),
-            pltpu.VMEM((KX * 2 * TILE, TILE), F32),
-            pltpu.VMEM((48, slabs * TILE), half_type),
-            pltpu.VMEM((48, slabs * TILE), half_type),
+            pltpu.VMEM((blocks, TILE, DEPTH), HALF),
+            pltpu.VMEM((blocks, DEPTH, 3 * TILE), HALF),
+            pltpu.VMEM((blocks, DEPTH, 3 * TILE), HALF),
+            pltpu.VMEM((KO * TILE, 3 * TILE), F32),
+            pltpu.VMEM((KO * TILE, 3 * TILE), F32),
+            pltpu.VMEM((KX * TILE, 3 * TILE), F32),
+            pltpu.VMEM((KX * TILE, 3 * TILE), F32),
+            pltpu.VMEM((48, slabs * TILE), HALF),
+            pltpu.VMEM((48, slabs * TILE), HALF),
+            pltpu.VMEM((PLANES, blocks, TILE), F32),
             dma((slabs,)),
             dma((slabs,)),
             dma((slabs,)),
@@ -481,10 +489,10 @@
     density, potential = pl.pallas_call(
         final_kernel,
         out_shape=(grid_shape, grid_shape),
-        in_specs=[VMEM, VMEM, VMEM, SMEM, SMEM],
+        in_specs=[VMEM, VMEM, VMEM, VMEM, SMEM, SMEM],
         out_specs=(VMEM, VMEM),
         scratch_shapes=[pltpu.VMEM((blocks + 8, TILE), F32)],
-    )(density, back, table, block_counts, group_owner)
+    )(particles[1], density, back, table, block_counts, group_owner)
     return (density.reshape(1, row_count), potential.reshape(1, row_count), energy)
 
 

time: 36.1 us -> 33.1 us (0.917)
  the two profiles are of different devices: /device:TPU:0 before, /device:TPU:1 now
where the time goes in v1:
time: 33.1 us; the launch traced here: 32.8 us
  Pallas kernels  30.3 us (92%)
  between operations  2.46 us (7%)
    pallas_call x1, Pallas kernels, per_device(): pl.pallas_call(functools.partial(main_kernel, slabs, grps), out_shape=(gr...  27.1 us
    pallas_call x1, Pallas kernels, per_device(): pl.pallas_call(pick_kernel, out_shape=jax.ShapeDtypeStruct((groups, 8, TI...  1.7 us
    pallas_call x1, Pallas kernels, per_device(): pl.pallas_call(final_kernel, out_shape=(grid_shape, grid_shape), in_specs...  1.56 us

profile of v1, /device:TPU:1, one launch (start us, length us, event | category | flops | bytes accessed | tf_op | source)
XLA Modules:
  0.0 32.8 jit_solution(13538616817155499794)
XLA Ops:
  0.6 1.7 %shard_map.85.group_ref = f32[8,8,128]{2,1,0:T(8,128)} custom-call(f32[3,64,128]{2,1,0:T(8,128)} %bitcast.8, f32[64,128]{1,0:T(8,128)} %bitcast.10, f32[64,128]{1,0:T(8,128)} %bitcast.13, s32[1,8]{1,0:T(1,128)} %count_ref.3, s32[1,8]{1,0:T(1,128)} %owner_ref.3), custom_call_target="tpu_custom_call" | custom-call | tf_op jit(solution)/shard_map/pallas_call | solution.py:445
  2.3 27.1 %shard_map.86 = (f32[64,128]{1,0:T(8,128)}, f32[8,1,128]{2,1,0:T(1,128)}, f32[64,128]{1,0:T(8,128)}, f32[1,1]{1,0:T(1,128)}) custom-call(f32[3,64,128]{2,1,0:T(8,128)} %bitcast.9, f32[64,128]{1,0:T(8,128)} %bitcast.11, f32[64,128]{1,0:T(8,128)} %bitcast.14, f32[8,8,128]{2,1,0:T(8,128)} %shard_map.85.group_ref, s32[8,64]{1,0:T(8,128)} %bitcast.15), custom_call_target="tpu_custom_call" | custom-call | tf_op jit(solution)/shard_map/pallas_call | solution.py:455
  29.4 1.6 %shard_map.87 = (f32[64,128]{1,0:T(8,128)}, f32[64,128]{1,0:T(8,128)}) custom-call(f32[64,128]{1,0:T(8,128)} %bitcast.12, f32[64,128]{1,0:T(8,128)} %get-tuple-element.9.dens_ref, f32[64,128]{1,0:T(8,128)} %get-tuple-element.10.back_ref, f32[8,1,128]{2,1,0:T(1,128)} %get-tuple-element.11.table_ref, s32[1,8]{1,0:T(1,128)} %count_ref.3, s32[1,8]{1,0:T(1,128)} %owner_ref.3), custom_call_target="tpu_custom_call" | custom-call | tf_op jit(solution)/shard_map/pallas_call | solution.py:489

commit v2 on v1

--- a/solution.py
+++ b/solution.py
@@ -126,8 +126,8 @@
     )
 
 
-def weights(both_ref, k):
-    rows = pl.ds(k * TILE, TILE)
+def weights(both_ref, base):
+    rows = pl.ds(base, 8)
     squared = jnp.maximum(both_ref[rows, :TILE], 1e-30)
     reach = both_ref[rows, TILE : 2 * TILE]
     near = jnp.maximum(reach - squared * lax.rsqrt(squared), 0.0)
@@ -136,18 +136,20 @@
     return (a * a) * (1.25 * reach - near)
 
 
-def sweep(first, last, fetch, use, even_ref, odd_ref, unroll=4):
-    fetch(first, even_ref)
-
+def sweep(first, last, end, fetch, use, even_ref, odd_ref, unroll):
     def step(i, _):
         b = first + 2 * i
         fetch(b + 1, odd_ref)
         use(b, even_ref)
-        fetch(jnp.minimum(b + 2, last - 1), even_ref)
+        fetch(jnp.minimum(b + 2, end - 1), even_ref)
         use(b + 1, odd_ref)
         return 0
 
     lax.fori_loop(0, (last - first) // 2, step, 0, unroll=unroll)
+
+
+def steps_of(first, last, most):
+    return math.gcd((last - first) // 2, most)
 
 
 def own_part(first, last, list_ref, dens_ref, left_ref, right_ref, even_ref, odd_ref):
@@ -158,11 +160,13 @@
 
     def use(b, both_ref):
         total = jnp.zeros((8, TILE), F32)
-        for k in range(KO):
-            total = total + jnp.sum(weights(both_ref, k).reshape(TILE // 8, 8, TILE), axis=0)
+        for base in range(0, KO * TILE, 8):
+            total = total + weights(both_ref, base)
         dens_ref[pl.ds(b, 1), :] += jnp.sum(total, axis=0, keepdims=True)
 
-    sweep(first, last, fetch, use, even_ref, odd_ref)
+    if first == 0:
+        fetch(0, even_ref)
+    sweep(first, last, left_ref.shape[0], fetch, use, even_ref, odd_ref, steps_of(first, last, 12 if (last - first) % 3 == 0 else 8))
 
 
 def cross_part(list_ref, dens_ref, column_ref, back_ref, left_ref, right_ref, even_ref, odd_ref):
@@ -174,14 +178,19 @@
             both_ref[pl.ds(k * TILE, TILE), :] = pair_dot(left, right_ref[list_ref[KX + KO + k, b]], 1)
 
     def use(b, both_ref):
-        total = None
+        column = [jnp.zeros((8, TILE), F32)] * KX
+        total = []
+        for base in range(0, TILE, 8):
+            values = [weights(both_ref, k * TILE + base) for k in range(KX)]
+            column = [old + value for old, value in zip(column, values)]
+            total.append(sum(values))
         for k in range(KX):
-            value = weights(both_ref, k)
-            total = value if total is None else total + value
-            column_ref[pl.ds(KX * b + k, 1), :] = jnp.sum(value, axis=0, keepdims=True)
+            column_ref[pl.ds(KX * b + k, 1), :] = jnp.sum(column[k], axis=0, keepdims=True)
+        total = jnp.concatenate(total, axis=0)
         dens_ref[pl.ds(b, 1), :] += jnp.sum(total.T, axis=0, keepdims=True)
 
-    sweep(0, blocks, fetch, use, even_ref, odd_ref)
+    fetch(0, even_ref)
+    sweep(0, blocks, blocks, fetch, use, even_ref, odd_ref, steps_of(0, blocks, 8))
 
     lane = lax.broadcasted_iota(jnp.int32, (1, KX * blocks), 1)
 
@@ -263,7 +272,7 @@
     parts = (place_ref, weight_ref, size_ref)
     far_parts = (far_place_ref, far_weight_ref, far_size_ref)
     blocks = dens_ref.shape[0]
-    early = blocks // 8 * 2
+    early = blocks // 16 * 2
     later = blocks // 4 * 2
     own = (list_ref, dens_ref, left_ref, right_ref, even_ref, odd_ref)
     dens_ref[...] = jnp.zeros_like(dens_ref)
@@ -324,17 +333,17 @@
 
     own_part(early, later, *own)
 
+    member_ref[slab] = group_ref[slab]
+    each(lambda d: member_copy(d).wait())
+    phi_part(member_ref, phi_ref, energy_ref, phi_target_ref, phi_source_ref)
+    each(lambda d: phi_copy(d).start())
+    table_ref[slab] = phi_ref[slab]
+
     for copy in part_copies:
         copy.wait()
     fill(far_parts, plane_ref, None, far_ref, 1.0)
     cross_part(list_ref, dens_ref, column_ref, sent_ref, left_ref, far_ref, near_even_ref, near_odd_ref)
     back_copy.start()
-
-    member_ref[slab] = group_ref[slab]
-    each(lambda d: member_copy(d).wait())
-    phi_part(member_ref, phi_ref, energy_ref, phi_target_ref, phi_source_ref)
-    each(lambda d: phi_copy(d).start())
-    table_ref[slab] = phi_ref[slab]
 
     own_part(later, blocks, *own)
     each(lambda d: phi_copy(d).wait())

time: 33.1 us -> 32.2 us (0.973)
  the two profiles are of different devices: /device:TPU:1 before, /device:TPU:0 now
where the time goes in v2:
time: 32.2 us; the launch traced here: 32 us
  Pallas kernels  29.5 us (92%)
  between operations  2.46 us (8%)
    pallas_call x1, Pallas kernels, per_device(): pl.pallas_call(functools.partial(main_kernel, slabs, grps), out_shape=(gr...  26.2 us
    pallas_call x1, Pallas kernels, per_device(): pl.pallas_call(pick_kernel, out_shape=jax.ShapeDtypeStruct((groups, 8, TI...  1.7 us
    pallas_call x1, Pallas kernels, per_device(): pl.pallas_call(final_kernel, out_shape=(grid_shape, grid_shape), in_specs...  1.56 us

profile of v2, /device:TPU:0, one launch (start us, length us, event | category | flops | bytes accessed | tf_op | source)
XLA Modules:
  0.0 32.0 jit_solution(17328817213627088177)
XLA Ops:
  0.6 1.7 %shard_map.85.group_ref = f32[8,8,128]{2,1,0:T(8,128)} custom-call(f32[3,64,128]{2,1,0:T(8,128)} %bitcast.8, f32[64,128]{1,0:T(8,128)} %bitcast.10, f32[64,128]{1,0:T(8,128)} %bitcast.13, s32[1,8]{1,0:T(1,128)} %count_ref.3, s32[1,8]{1,0:T(1,128)} %owner_ref.3), custom_call_target="tpu_custom_call" | custom-call | tf_op jit(solution)/shard_map/pallas_call | solution.py:454
  2.3 26.2 %shard_map.86 = (f32[64,128]{1,0:T(8,128)}, f32[8,1,128]{2,1,0:T(1,128)}, f32[64,128]{1,0:T(8,128)}, f32[1,1]{1,0:T(1,128)}) custom-call(f32[3,64,128]{2,1,0:T(8,128)} %bitcast.9, f32[64,128]{1,0:T(8,128)} %bitcast.11, f32[64,128]{1,0:T(8,128)} %bitcast.14, f32[8,8,128]{2,1,0:T(8,128)} %shard_map.85.group_ref, s32[8,64]{1,0:T(8,128)} %bitcast.15), custom_call_target="tpu_custom_call" | custom-call | tf_op jit(solution)/shard_map/pallas_call | solution.py:464
  28.6 1.6 %shard_map.87 = (f32[64,128]{1,0:T(8,128)}, f32[64,128]{1,0:T(8,128)}) custom-call(f32[64,128]{1,0:T(8,128)} %bitcast.12, f32[64,128]{1,0:T(8,128)} %get-tuple-element.9.dens_ref, f32[64,128]{1,0:T(8,128)} %get-tuple-element.10.back_ref, f32[8,1,128]{2,1,0:T(1,128)} %get-tuple-element.11.table_ref, s32[1,8]{1,0:T(1,128)} %count_ref.3, s32[1,8]{1,0:T(1,128)} %owner_ref.3), custom_call_target="tpu_custom_call" | custom-call | tf_op jit(solution)/shard_map/pallas_call | solution.py:498

commit v3 on v2

--- a/solution.py
+++ b/solution.py
@@ -117,7 +117,7 @@
             right_ref[i, :, pl.ds(m * TILE, TILE)] = jnp.concatenate(column, axis=0).astype(HALF)
         return 0
 
-    lax.fori_loop(0, right_ref.shape[0], step, 0, unroll=4)
+    lax.fori_loop(0, right_ref.shape[0], step, 0, unroll=8)
 
 
 def pair_dot(left, right, left_dim=0):
@@ -214,8 +214,9 @@
     place_ref,
     weight_ref,
     size_ref,
-    group_ref,
     list_ref,
+    count_ref,
+    owner_ref,
     dens_ref,
     table_ref,
     back_ref,
@@ -223,6 +224,7 @@
     far_place_ref,
     far_weight_ref,
     far_size_ref,
+    group_ref,
     member_ref,
     phi_ref,
     column_ref,
@@ -277,6 +279,7 @@
     own = (list_ref, dens_ref, left_ref, right_ref, even_ref, odd_ref)
     dens_ref[...] = jnp.zeros_like(dens_ref)
     fill(parts, plane_ref, left_ref, right_ref, 0.0)
+    pick_groups(parts, count_ref, owner_ref, group_ref)
     own_part(0, early, *own)
     pl.semaphore_wait(barrier, slabs + 1)
 
@@ -333,17 +336,17 @@
 
     own_part(early, later, *own)
 
+    for copy in part_copies:
+        copy.wait()
+    fill(far_parts, plane_ref, None, far_ref, 1.0)
+    cross_part(list_ref, dens_ref, column_ref, sent_ref, left_ref, far_ref, near_even_ref, near_odd_ref)
+    back_copy.start()
+
     member_ref[slab] = group_ref[slab]
     each(lambda d: member_copy(d).wait())
     phi_part(member_ref, phi_ref, energy_ref, phi_target_ref, phi_source_ref)
     each(lambda d: phi_copy(d).start())
     table_ref[slab] = phi_ref[slab]
-
-    for copy in part_copies:
-        copy.wait()
-    fill(far_parts, plane_ref, None, far_ref, 1.0)
-    cross_part(list_ref, dens_ref, column_ref, sent_ref, left_ref, far_ref, near_even_ref, near_odd_ref)
-    back_copy.start()
 
     own_part(later, blocks, *own)
     each(lambda d: phi_copy(d).wait())
@@ -360,24 +363,26 @@
     return block
 
 
-def pick_kernel(place_ref, weight_ref, size_ref, count_ref, owner_ref, out_ref):
-    parts = (place_ref, weight_ref, size_ref)
-    blocks = weight_ref.shape[0]
+def pick_groups(parts, count_ref, owner_ref, group_ref):
+    blocks = parts[1].shape[0]
     row = lax.broadcasted_iota(jnp.int32, (8, TILE), 0)
     lane = lax.broadcasted_iota(jnp.int32, (8, TILE), 1)
+    slot = lax.broadcasted_iota(jnp.int32, group_ref.shape, 0)
 
     def step(k, start):
         count = count_ref[0, k]
         block = jnp.minimum(start // TILE, blocks - 1)
         shift = start % TILE
-        after = jnp.minimum(block + 1, blocks - 1)
         first = block_of(parts, block)
-        second = block_of(parts, after)
+        second = block_of(parts, jnp.minimum(block + 1, blocks - 1))
         mixed = pltpu.roll(jnp.where(lane >= shift, first, second), (TILE - shift) % TILE, 1)
-        out_ref[owner_ref[0, k]] = jnp.where((row == 3) & (lane >= count), 0.0, mixed)
+        mixed = jnp.where((row == 3) & (lane >= count), 0.0, mixed)
+        group_ref[...] = jnp.where(slot == owner_ref[0, k], mixed, group_ref[...])
         return start + count
 
-    lax.fori_loop(0, count_ref.shape[1], step, jnp.int32(0), unroll=8)
+    group_ref[...] = jnp.zeros_like(group_ref)
+    groups = count_ref.shape[1]
+    lax.fori_loop(0, groups, step, jnp.int32(0), unroll=math.gcd(groups, 8))
 
 
 def phi_part(member_ref, phi_ref, energy_ref, target_ref, source_ref):
@@ -421,7 +426,8 @@
     energy_ref[...] = 0.5 * jnp.sum(energy, axis=1, keepdims=True)
 
 
-def final_kernel(mass_ref, dens_ref, back_ref, table_ref, count_ref, owner_ref, out_ref, pot_ref, work_ref):
+def final_kernel(mass_ref, dens_ref, back_ref, table_ref, energy_ref, count_ref, owner_ref, out_ref, pot_ref, total_ref, work_ref):
+    total_ref[...] = energy_ref[...]
     out_ref[...] = (dens_ref[...] + back_ref[...]) * (DENSITY_SCALE / mass_ref[...])
     work_ref[...] = jnp.zeros_like(work_ref)
     lane = lax.broadcasted_iota(jnp.int32, (1, TILE), 1)
@@ -443,7 +449,6 @@
 def per_device(positions, masses, smoothing, block_lists, block_counts, group_owner):
     row_count = masses.shape[1]
     blocks = row_count // TILE
-    groups = block_counts.shape[1]
     slabs = lax.axis_size("slab")
     grps = lax.axis_size("grp")
     particles = (
@@ -451,25 +456,19 @@
         masses.reshape(blocks, TILE),
         smoothing.reshape(blocks, TILE),
     )
-    outgoing = pl.pallas_call(
-        pick_kernel,
-        out_shape=jax.ShapeDtypeStruct((groups, 8, TILE), F32),
-        in_specs=[VMEM, VMEM, VMEM, SMEM, SMEM],
-        out_specs=VMEM,
-    )(*particles, block_counts, group_owner)
-
     grid_shape = jax.ShapeDtypeStruct((blocks, TILE), F32)
     row_shape = jax.ShapeDtypeStruct((slabs, 1, TILE), F32)
     dma = pltpu.SemaphoreType.DMA
     density, table, back, energy = pl.pallas_call(
         functools.partial(main_kernel, slabs, grps),
         out_shape=(grid_shape, row_shape, grid_shape, jax.ShapeDtypeStruct((1, 1), F32)),
-        in_specs=[VMEM, VMEM, VMEM, VMEM, SMEM],
+        in_specs=[VMEM, VMEM, VMEM, SMEM, SMEM, SMEM],
         out_specs=(VMEM, VMEM, VMEM, VMEM),
         scratch_shapes=[
             pltpu.VMEM((3, blocks, TILE), F32),
             pltpu.VMEM((blocks, TILE), F32),
             pltpu.VMEM((blocks, TILE), F32),
+            pltpu.VMEM((slabs, 8, TILE), F32),
             pltpu.VMEM((slabs, 8, TILE), F32),
             pltpu.VMEM((slabs, 1, TILE), F32),
             pltpu.VMEM((KX * blocks, TILE), F32),
@@ -494,14 +493,14 @@
             dma,
         ],
         compiler_params=pltpu.CompilerParams(collective_id=0, has_side_effects=True),
-    )(*particles, outgoing, block_lists[0].T)
-    density, potential = pl.pallas_call(
+    )(*particles, block_lists[0].T, block_counts, group_owner)
+    density, potential, energy = pl.pallas_call(
         final_kernel,
-        out_shape=(grid_shape, grid_shape),
-        in_specs=[VMEM, VMEM, VMEM, VMEM, SMEM, SMEM],
-        out_specs=(VMEM, VMEM),
+        out_shape=(grid_shape, grid_shape, jax.ShapeDtypeStruct((1, 1), F32)),
+        in_specs=[VMEM, VMEM, VMEM, VMEM, VMEM, SMEM, SMEM],
+        out_specs=(VMEM, VMEM, VMEM),
         scratch_shapes=[pltpu.VMEM((blocks + 8, TILE), F32)],
-    )(particles[1], density, back, table, block_counts, group_owner)
+    )(particles[1], density, back, table, energy, block_counts, group_owner)
     return (density.reshape(1, row_count), potential.reshape(1, row_count), energy)
 
 

time: 32.2 us -> 29.1 us (0.904)
  between operations: 2.46 us -> 0.64 us
  Pallas kernels: 29.5 us -> 28.2 us
    pallas_call x2 -> x1, Pallas kernels: 3.26 us -> 2.25 us  [per_device(): pl.pallas_call(final_kernel, out_shape=(grid_shape, grid_shape, jax.Shape...]
where the time goes in v3:
time: 29.1 us; the launch traced here: 28.8 us
  Pallas kernels  28.2 us (97%)
  between operations  0.64 us (2%)
    pallas_call x1, Pallas kernels, per_device(): pl.pallas_call(functools.partial(main_kernel, slabs, grps), out_shape=(gr...  25.9 us
    pallas_call x1, Pallas kernels, per_device(): pl.pallas_call(final_kernel, out_shape=(grid_shape, grid_shape, jax.Shape...  2.25 us

profile of v3, /device:TPU:0, one launch (start us, length us, event | category | flops | bytes accessed | tf_op | source)
XLA Modules:
  0.0 28.8 jit_solution(8624577465133761672)
XLA Ops:
  0.6 25.9 %shard_map.85 = (f32[64,128]{1,0:T(8,128)}, f32[8,1,128]{2,1,0:T(1,128)}, f32[64,128]{1,0:T(8,128)}, f32[1,1]{1,0:T(1,128)}) custom-call(f32[3,64,128]{2,1,0:T(8,128)} %bitcast.10, f32[64,128]{1,0:T(8,128)} %bitcast.8, f32[64,128]{1,0:T(8,128)} %bitcast.11, s32[8,64]{1,0:T(8,128)} %bitcast.12, s32[1,8]{1,0:T(1,128)} %count_ref.3, s32[1,8]{1,0:T(1,128)} %owner_ref.3), custom_call_target="tpu_custom_call" | custom-call | tf_op jit(solution)/shard_map/pallas_call | solution.py:462
  26.6 2.3 %shard_map.86 = (f32[64,128]{1,0:T(8,128)}, f32[64,128]{1,0:T(8,128)}, f32[1,1]{1,0:T(1,128)}) custom-call(f32[64,128]{1,0:T(8,128)} %bitcast.9, f32[64,128]{1,0:T(8,128)} %get-tuple-element.10.dens_ref, f32[64,128]{1,0:T(8,128)} %get-tuple-element.11.back_ref, f32[8,1,128]{2,1,0:T(1,128)} %get-tuple-element.12.table_ref, ...), custom_call_target="tpu_custom_call" | custom-call | tf_op jit(solution)/shard_map/pallas_call | solution.py:497
